TPU v7x, 512 devices: a whole 4x4x16 slice. The times are simulated.
512 devices in a mesh: req: 128 (over x, z, core), tp: 4 (over y).
Axes of the slice: x: 4, y: 4, z: 16, core: 2. Of those that a mesh axis runs over, the one named last changes fastest.
Arguments:
- queries: bfloat16 [2, 128, 32, 1536], P(None, 'req', None, 'tp')
- response_kv: bfloat16 [2, 128, 2, 32, 256], P(None, 'req'), may hold values from -6 to 6
- cache_kv: bfloat16 [2, 128, 2, 384, 256], P(None, 'req'), may hold values from -6 to 6
- residual: bfloat16 [2, 128, 32, 1536], P(None, 'req')
- out_proj: bfloat16 [2, 1536, 1536], P(None, 'tp'), may hold values from -0.5 to 0.5
- norm_gain: float32 [2, 1536], replicated, may hold values from 0.25 to 1.75
- lm_head: bfloat16 [2, 131072, 1536], P(None, 'req', 'tp')
- targets: int32 [128, 32], P(None, 'tp'), may hold values from 0 to 131071
- resp_lengths: int32 [128], replicated, may hold values from 1 to 32, 2560 in all
- cache_lengths: int32 [128], P('req'), may hold values from 1 to 384, 30720 in all
- owner_slot: int32 [128], replicated, may hold values from 0 to 127, each once
- sink_count: int32 [1], replicated, may hold values from 1 to 95
- window_size: int32 [1], replicated, may hold values from 48 to 191
Outputs:
- token_logprobs: float32 [128, 32], P('req', 'tp')
- request_scores: float32 [128, 2], P('req')
Inputs may be any that keep to these rules, and one draw needn't show every extreme that they name: `resp_lengths`: live response slots are the first ones; all lengths sum to 2560. `cache_lengths`: live cache slots are the first ones; all lengths sum to 30720. `owner_slot`: A permutation of the requests.
All inputs are finite; a program needn't handle non-finite values. No bound on the sum of `cache_lengths` on one device may be relied on, other than what follows from the above.
Results may differ from a plain program's by a relative error of at most 0.0014.
Values may be sent and summed in bfloat16 or wider, within the bound.
A program may use at most 128 MiB of HBM per device.

v0:
```python
import jax
import jax.numpy as jnp
from jax import lax
from jax.sharding import PartitionSpec as P

HEADS = 12
HEAD = 128
KV_HEADS = 2
RESP = 32
CACHE = 384


def span_mask(lengths, sink_count, window_size):
    cache_pos = jnp.arange(CACHE, dtype=jnp.int32)
    slot_pos = jnp.arange(RESP, dtype=jnp.int32)
    req_count = lengths.shape[0]
    key_pos = jnp.concatenate([cache_pos[None, :], lengths[:, None] + slot_pos[None, :]], axis=1)
    key_live = jnp.concatenate(
        [cache_pos[None, :] < lengths[:, None], jnp.ones((req_count, RESP), jnp.bool_)], axis=1
    )
    query_pos = lengths[:, None] + slot_pos[None, :]
    earlier = key_pos[:, None, :] <= query_pos[:, :, None]
    inside = (key_pos[:, None, :] < sink_count[0]) | (
        query_pos[:, :, None] - key_pos[:, None, :] < window_size[0]
    )
    return key_live[:, None, :] & earlier & inside


def rms_norm(hidden, norm_gain):
    scale_inv = lax.rsqrt(jnp.mean(hidden * hidden, axis=-1, keepdims=True) + 1e-06)
    return (hidden * scale_inv * norm_gain[:, None, None, :]).astype(jnp.bfloat16)


def per_device(
    queries,
    response_kv,
    cache_kv,
    residual,
    out_proj,
    norm_gain,
    lm_head,
    targets,
    resp_lengths,
    cache_lengths,
    owner_slot,
    sink_count,
    window_size,
):
    tp_size = lax.axis_size("tp")
    tp_index = lax.axis_index("tp")
    req_index = lax.axis_index("req")
    local_reqs = queries.shape[1]
    local_heads = HEADS // tp_size
    group_size = HEADS // KV_HEADS
    kv_index = tp_index * local_heads // group_size
    quarter = RESP // tp_size
    cache_head = lax.dynamic_slice_in_dim(cache_kv, kv_index * HEAD, HEAD, axis=4)
    resp_head = lax.dynamic_slice_in_dim(response_kv, kv_index * HEAD, HEAD, axis=4)
    key_rows = jnp.concatenate([cache_head[:, :, 0], resp_head[:, :, 0]], axis=2)
    value_rows = jnp.concatenate([cache_head[:, :, 1], resp_head[:, :, 1]], axis=2)
    query_heads = queries.reshape(2, local_reqs, RESP, local_heads, HEAD)
    scores = jnp.einsum(
        "mrshd,mrkd->mrhsk", query_heads, key_rows, preferred_element_type=jnp.float32
    ) * HEAD ** (-0.5)
    allowed = span_mask(cache_lengths, sink_count, window_size)[None, :, None]
    masked = jnp.where(allowed, scores, -jnp.inf)
    row_peak = jnp.max(masked, axis=-1, keepdims=True)
    weights = jnp.exp(masked - row_peak)
    weights = (weights / jnp.sum(weights, axis=-1, keepdims=True)).astype(jnp.bfloat16)
    attended = jnp.einsum(
        "mrhsk,mrkd->mrshd", weights, value_rows, preferred_element_type=jnp.float32
    )
    attended = attended.astype(jnp.bfloat16).reshape(2, local_reqs, RESP, local_heads * HEAD)
    partial_value = jnp.einsum(
        "mrsf,mfd->mrsd", attended, out_proj, preferred_element_type=jnp.float32
    )
    start_slot = tp_index * quarter
    projected = lax.dynamic_slice_in_dim(lax.psum(partial_value, "tp"), start_slot, quarter, axis=2)
    own_residual = lax.dynamic_slice_in_dim(residual, start_slot, quarter, axis=2)
    hidden = own_residual.astype(jnp.float32) + projected
    normed = rms_norm(hidden, norm_gain)
    flat_rows = normed.reshape(2, local_reqs * quarter, normed.shape[3])
    full_head = lax.all_gather(lm_head, "tp", axis=2, tiled=True)
    vocab_rows = full_head.shape[1]
    vocab_start = req_index * vocab_rows
    flat_targets = targets.reshape(-1)
    total_rows = flat_targets.shape[0]
    requests = total_rows // quarter
    logits = jnp.einsum(
        "mnd,mvd->mnv",
        lax.all_gather(flat_rows, "req", axis=1, tiled=True),
        full_head,
        preferred_element_type=jnp.float32,
    )
    block_peak = jnp.max(logits, axis=-1)
    block_total = jnp.sum(jnp.exp(logits - block_peak[..., None]), axis=-1)
    wanted = flat_targets - vocab_start
    target_hits = jnp.arange(vocab_rows, dtype=jnp.int32)[None, None, :] == wanted[None, :, None]
    block_pick = jnp.sum(jnp.where(target_hits, logits, 0.0), axis=-1)
    peak_all = block_peak
    total_all = block_total
    picked_all = block_pick
    peak_all = peak_all.reshape(2, requests, quarter)
    total_all = total_all.reshape(2, requests, quarter)
    picked_all = picked_all.reshape(2, requests, quarter)
    row_order = (
        jnp.zeros((requests,), jnp.int32).at[owner_slot].set(jnp.arange(requests, dtype=jnp.int32))
    )
    owned_reqs = lax.dynamic_slice_in_dim(row_order, req_index * local_reqs, local_reqs)
    vocab_top = lax.pmax(peak_all, "req")
    exp_total, picked = lax.psum((total_all * jnp.exp(peak_all - vocab_top), picked_all), "req")
    logprob = (picked - (vocab_top + jnp.log(exp_total)))[:, owned_reqs]
    lengths_owned = resp_lengths[owned_reqs]
    live_slots = (start_slot + jnp.arange(quarter, dtype=jnp.int32))[None, :] < lengths_owned[
        :, None
    ]
    policy = jnp.where(live_slots, logprob[0], 0.0)
    log_ratio = jnp.where(live_slots, logprob[0] - logprob[1], 0.0)
    policy_total, ratio_total = lax.psum(
        (jnp.sum(policy, axis=1), jnp.sum(log_ratio, axis=1)), "tp"
    )
    counts = lengths_owned.astype(jnp.float32)
    request_scores = jnp.stack([policy_total / counts, ratio_total / counts], axis=1)
    return (policy, request_scores)


def solution(mesh):
    in_specs = (
        P(None, "req", None, "tp"),
        P(None, "req", None, None, None),
        P(None, "req", None, None, None),
        P(None, "req", None, None),
        P(None, "tp", None),
        P(),
        P(None, "req", "tp"),
        P(None, "tp"),
        P(),
        P("req"),
        P(),
        P(),
        P(),
    )
    out_specs = (P("req", "tp"), P("req", None))
    return jax.shard_map(
        per_device, mesh=mesh, in_specs=in_specs, out_specs=out_specs, check_vma=False
    )
```

profile of v0, /device:TPU:8, one launch (start us, length us, event | category | flops | bytes accessed | tf_op | source)
XLA Modules:
  0.0 1325.8 jit_solution(16412632593061100903)
XLA Ops:
  7.3 1.2 dynamic-slice_bitcast_fusion
  8.5 0.8 dynamic-slice_bitcast_fusion.2
  11.3 0.8 reshape.303
  12.2 0.3 fusion.23
  13.2 1.3 convolution_bitcast_fusion
  14.5 0.7 all-gather.4.cloned.1.call-update
  15.3 60.6 %all-reduce.5.cloned.1.call-done = f32[2,1,32,1536]{3,2,0,1:T(8,128)} async-done(((f32[2,1,32,1536]{3,2,0,1:T(8,128)}), f32[2,1,32,1536]{3,2,0,1:T(8,128)}) %all-reduce.5.cloned.1.call-update) | async-done | bytes 393232 | tf_op jit(solution)/shard_map/psum | solution.py:78
  75.8 1.0 multiply_reduce_fusion
  76.9 1.6 multiply_convert_fusion
  78.7 1.0 scatter_custom_fusion
  79.7 0.6 dynamic_slice.15
  82.2 0.6 dynamic-slice.5
  83.5 0.8 iota_compare_fusion
  84.3 68.4 %all-gather.4.cloned.1.call-done = bf16[2,1024,1536]{2,1,0:T(8,128)(2,1)} async-done(((bf16[2,1024,384]{2,1,0:T(8,128)(2,1)}), bf16[2,1024,1536]{2,1,0:T(8,128)(2,1)}) %all-gather.4.cloned.1.call-update) | async-done | bytes 6291472 | tf_op jit(solution)/shard_map/all_gather | solution.py:83
  152.7 149.5 %all-gather.6.cloned.1.call-done = bf16[2,1,1024,1536]{3,2,0,1:T(8,128)(2,1)} async-done(((bf16[2,1,8,1536]{3,2,0,1:T(8,128)(2,1)}), bf16[2,1,1024,1536]{3,2,0,1:T(8,128)(2,1)}) %all-gather.6.cloned.1.call-update) | async-done | bytes 6291472 | tf_op jit(solution)/shard_map/all_gather | solution.py:91
  302.2 12.7 fusion.24
  315.0 5.1 exponential_reduce_fusion
  320.1 0.8 reshape.309
  320.9 493.2 %pmax.7 = f32[2,128,8]{2,1,0:T(8,128)S(1)} all-reduce(f32[2,128,8]{2,1,0:T(8,128)S(1)} %reshape.308), channel_id=1, replica_groups=mesh['req'=128,'tp'=4] {'req'}, use_global_device_ids=true, to_apply=%region_8.9 | all-reduce | flops 2048 | bytes 16384 | tf_op jit(solution)/shard_map/pmax | solution.py:110
  814.2 490.9 %all-reduce.1 = (f32[2,128,8]{2,1,0:T(8,128)S(1)}, f32[2,128,8]{2,1,0:T(8,128)S(1)}) all-reduce(f32[2,128,8]{2,1,0:T(8,128)S(1)} %reshape.307, f32[2,128,8]{2,1,0:T(8,128)S(1)} %exponential_multiply_fusion), channel_id=1, replica_groups=mesh['req'=128,'tp'=4] {'req'}, use_global_device_ids=true, to_apply=%region_6.7 | all-reduce | flops 4096 | bytes 32768 | tf_op jit(solution)/shard_map/psum | solution.py:111
  1305.2 1.2 fusion.17
  1306.4 1.7 fusion.22
  1308.1 9.3 all-reduce.2
  1318.7 0.6 pad_maximum_fusion
  (39 shorter events, 1.4 us)
Async XLA Ops:
  7.2 6.0 copy-start
  7.2 68.7 %copy-start.1 = (bf16[2,1,32,1536]{3,2,1,0:T(8,128)(2,1)S(1)}, bf16[2,1,32,1536]{3,2,1,0:T(8,128)(2,1)}, u32[]{:S(2)}) copy-start(bf16[2,1,32,1536]{3,2,1,0:T(8,128)(2,1)} %param.16) | copy-start | bytes 589828
  7.2 69.7 %copy-start.2 = (f32[2,1536]{1,0:T(2,128)S(1)}, f32[2,1536]{1,0:T(2,128)}, u32[]{:S(2)}) copy-start(f32[2,1536]{1,0:T(2,128)} %param.18) | copy-start | bytes 36868
  7.2 71.3 %copy-start.3 = (s32[128,8]{0,1:T(8,128)S(1)}, s32[128,8]{0,1:T(8,128)}, u32[]{:S(2)}) copy-start(s32[128,8]{0,1:T(8,128)} %param.20) | copy-start | bytes 12292
  7.2 71.5 %copy-start.4 = (s32[128]{0:T(128)S(1)}, s32[128]{0:T(128)}, u32[]{:S(2)}) copy-start(s32[128]{0:T(128)} %param.23) | copy-start | bytes 1540
  7.2 75.0 %copy-start.5 = (s32[128]{0:T(128)S(1)}, s32[128]{0:T(128)}, u32[]{:S(2)}) copy-start(s32[128]{0:T(128)} %param.21) | copy-start | bytes 1540
  7.2 68.6 %all-reduce.5.cloned.1.call-start = ((), (), s32[]{:S(2)}) async-start(), calls=%async_computation | async-start | bytes 786432 | tf_op jit(solution)/shard_map/psum | solution.py:78
  14.4 138.2 %all-gather.4.cloned.1.call-start = ((), (), s32[]{:S(2)}) async-start(), calls=%async_computation.1 | async-start | bytes 7864320 | tf_op jit(solution)/shard_map/all_gather | solution.py:83
  15.2 287.0 %all-gather.6.cloned.1.call-start = ((), (), s32[]{:S(2)}) async-start(), calls=%async_computation.2 | async-start | bytes 6340608 | tf_op jit(solution)/shard_map/all_gather | solution.py:91
Sparse Core Ops, SparseCore 0:
  14.6 61.2 all-reduce.4
  78.2 74.4 all-gather.3
  156.4 145.7 all-gather.5
where the time goes:
time: 1330 us
  blocking collectives  993 us (75%)
  waiting for transfers between devices  279 us (21%)
  between operations  19.9 us (1%)
  matrix products  14.6 us (1%)
    pmax x1, blocking collectives, per_device(): vocab_top = lax.pmax(peak_all, 'req')  493 us
    psum x1, blocking collectives, per_device(): lax.psum((total_all * jnp.exp(peak_all - vocab_top), picked_all), 'req')  491 us
    all_gather x1, waiting for transfers between devices, per_device(): lax.all_gather(flat_rows, 'req', axis=1, tiled=True)  149 us
    all_gather x1, waiting for transfers between devices, per_device(): full_head = lax.all_gather(lm_head, 'tp', axis=2, tiled=True)  68.4 us
    psum x1, waiting for transfers between devices, per_device(): lax.psum(partial_value, 'tp')  60.6 us
  transfers between devices with their start and end apart: 3, of which 3 were waited for; matrix products, arithmetic and copies ran while one was open for 0% of the time, Pallas kernels for 0%

commit v1 on v0

--- a/solution.py
+++ b/solution.py
@@ -80,7 +80,12 @@
     hidden = own_residual.astype(jnp.float32) + projected
     normed = rms_norm(hidden, norm_gain)
     flat_rows = normed.reshape(2, local_reqs * quarter, normed.shape[3])
-    full_head = lax.all_gather(lm_head, "tp", axis=2, tiled=True)
+    ring = [lm_head]
+    for hop in range(3):
+        ring.append(lax.ppermute(ring[-1], "tp", [(dev, (dev + 1) % 4) for dev in range(4)]))
+    full_head = jnp.roll(
+        jnp.concatenate(ring[::-1], axis=2), (lax.axis_index("tp") + 1) * ring[0].shape[2], axis=2
+    )
     vocab_rows = full_head.shape[1]
     vocab_start = req_index * vocab_rows
     flat_targets = targets.reshape(-1)

time: 1330 us -> 1250 us (0.940)
  waiting for transfers between devices: 279 us -> 172 us
  local copies, waits for them, and re-layouts: 6.31 us -> 25.5 us
    all_gather x1, waiting for transfers between devices: 149 us -> 20.8 us  [per_device(): lax.all_gather(flat_rows, 'req', axis=1, tiled=True)]
    ppermute x0 -> x3, waiting for transfers between devices: none -> 89.8 us  [per_device(): lax.ppermute(ring[-1], 'tp', [(dev, (dev + 1) % 4) for dev in range(4)])]
    all_gather x1 -> x0, waiting for transfers between devices: 68.4 us -> none  [per_device(): full_head = lax.all_gather(lm_head, 'tp', axis=2, tiled=True)]
    unnamed x12 -> x15, local copies, waits for them, and re-layouts: 0.03 us -> 17.2 us
  transfers between devices with their start and end apart: 3 -> 5, of which waited for: 3 -> 5; matrix products, arithmetic and copies ran while one was open for 0% -> 2% of each run, Pallas kernels for 0% -> 0%
where the time goes in v1:
time: 1250 us
  blocking collectives  993 us (79%)
  waiting for transfers between devices  172 us (14%)
  local copies, waits for them, and re-layouts  25.5 us (2%)
  between operations  20 us (2%)
  matrix products  14.7 us (1%)
  other arithmetic  13.7 us (1%)
    pmax x1, blocking collectives, per_device(): vocab_top = lax.pmax(peak_all, 'req')  493 us
    psum x1, blocking collectives, per_device(): lax.psum((total_all * jnp.exp(peak_all - vocab_top), picked_all), 'req')  491 us
    ppermute x3, waiting for transfers between devices, per_device(): lax.ppermute(ring[-1], 'tp', [(dev, (dev + 1) % 4) for dev in range(4)])  89.8 us
    psum x1, waiting for transfers between devices, per_device(): lax.psum(partial_value, 'tp')  61.3 us
  transfers between devices with their start and end apart: 5, of which 5 were waited for; matrix products, arithmetic and copies ran while one was open for 2% of the time, Pallas kernels for 0%

profile of v1, /device:TPU:8, one launch (start us, length us, event | category | flops | bytes accessed | tf_op | source)
XLA Modules:
  0.0 1249.5 jit_solution(1877286049161735090)
XLA Ops:
  13.1 1.3 convolution_bitcast_fusion
  14.4 61.3 %all-reduce.5.cloned.1.call-done = f32[2,1,32,1536]{3,2,0,1:T(8,128)} async-done(((f32[2,1,32,1536]{3,2,0,1:T(8,128)}), f32[2,1,32,1536]{3,2,0,1:T(8,128)}) %all-reduce.5.cloned.1.call-update) | async-done | bytes 393232 | tf_op jit(solution)/shard_map/psum | solution.py:78
  76.8 1.6 multiply_convert_fusion
  78.4 3.5 collective-permute-start
  81.9 32.7 %collective-permute-done = bf16[2,1024,384]{2,1,0:T(8,128)(2,1)S(1)} collective-permute-done((bf16[2,1024,384]{2,1,0:T(8,128)(2,1)}, bf16[2,1024,384]{2,1,0:T(8,128)(2,1)S(1)}, u32[]{:S(2)}, u32[]{:S(2)}) %collective-permute-start) | collective-permute-done | bytes 1572896 | tf_op jit(solution)/shard_map/ppermute | solution.py:85
  115.7 3.6 collective-permute-start.1
  119.3 32.3 %collective-permute-done.1 = bf16[2,1024,384]{2,1,0:T(8,128)(2,1)} collective-permute-done((bf16[2,1024,384]{2,1,0:T(8,128)(2,1)S(1)}, bf16[2,1024,384]{2,1,0:T(8,128)(2,1)}, u32[]{:S(2)}, u32[]{:S(2)}) %collective-permute-start.1) | collective-permute-done | bytes 1572896 | tf_op jit(solution)/shard_map/ppermute | solution.py:85
  151.6 3.0 collective-permute-start.2
  162.3 24.9 %collective-permute-done.2 = bf16[2,1024,384]{2,1,0:T(8,128)(2,1)} collective-permute-done((bf16[2,1024,384]{2,1,0:T(8,128)(2,1)}, bf16[2,1024,384]{2,1,0:T(8,128)(2,1)}, u32[]{:S(2)}, u32[]{:S(2)}) %collective-permute-start.2) | collective-permute-done | bytes 1572896 | tf_op jit(solution)/shard_map/ppermute | solution.py:85
  187.2 3.0 constant_dynamic-update-slice_fusion.7
  190.2 2.8 constant_dynamic-update-slice_fusion.6
  193.0 1.4 constant_dynamic-update-slice_fusion.5
  194.5 1.5 constant_dynamic-update-slice_fusion.4
  196.0 2.8 constant_dynamic-update-slice_fusion.3
  198.8 2.9 constant_dynamic-update-slice_fusion.2
  201.7 1.5 constant_dynamic-update-slice_fusion.1
  203.2 1.5 constant_dynamic-update-slice_fusion
  204.7 20.8 %all-gather.3.cloned.1.call-done = bf16[2,1,1024,1536]{3,2,0,1:T(8,128)(2,1)} async-done(((bf16[2,1,8,1536]{3,2,0,1:T(8,128)(2,1)}), bf16[2,1,1024,1536]{3,2,0,1:T(8,128)(2,1)}) %all-gather.3.cloned.1.call-update) | async-done | bytes 6291472 | tf_op jit(solution)/shard_map/all_gather | solution.py:96
  225.5 12.9 %fusion.26 = (f32[2,1024]{1,0:T(2,128)S(1)}, f32[2,1024,1024]{1,2,0:T(8,128)}) fusion(bf16[2,1024,3072]{2,1,0:T(8,128)(2,1)} %constant_dynamic-update-slice_fusion, s32[]{:T(128)S(6)} %select_n.69, bf16[2,1,1024,1536]{3,2,0,1:T(8,128)(2,1)} %all-gather.3.cloned.1.call-done), kind=kOutput, calls=%fused_computation.70 | convolution fusion | flops 6444546048 | bytes 20979716 | tf_op jit(solution)/shard_map/mnd,mvd->mnv/dot_general | solution.py:94
  238.5 5.1 exponential_reduce_fusion
  244.5 493.4 %pmax.7 = f32[2,128,8]{2,1,0:T(8,128)S(1)} all-reduce(f32[2,128,8]{2,1,0:T(8,128)S(1)} %reshape.308), channel_id=1, replica_groups=mesh['req'=128,'tp'=4] {'req'}, use_global_device_ids=true, to_apply=%region_8.9 | all-reduce | flops 2048 | bytes 16384 | tf_op jit(solution)/shard_map/pmax | solution.py:115
  737.9 490.9 %all-reduce.1 = (f32[2,128,8]{2,1,0:T(8,128)S(1)}, f32[2,128,8]{2,1,0:T(8,128)S(1)}) all-reduce(f32[2,128,8]{2,1,0:T(8,128)S(1)} %reshape.307, f32[2,128,8]{2,1,0:T(8,128)S(1)} %exponential_multiply_fusion), channel_id=1, replica_groups=mesh['req'=128,'tp'=4] {'req'}, use_global_device_ids=true, to_apply=%region_6.7 | all-reduce | flops 4096 | bytes 32768 | tf_op jit(solution)/shard_map/psum | solution.py:116
  1228.8 1.7 fusion.24
  1231.7 9.1 all-reduce.2
  (46 shorter events, 14.1 us)
Async XLA Ops:
  7.2 5.9 copy-start
  7.2 68.6 %all-reduce.5.cloned.1.call-start = ((), (), s32[]{:S(2)}) async-start(), calls=%async_computation | async-start | bytes 786432 | tf_op jit(solution)/shard_map/psum | solution.py:78
  14.4 211.1 %all-gather.3.cloned.1.call-start = ((), (), s32[]{:S(2)}) async-start(), calls=%async_computation.1 | async-start | bytes 6340608 | tf_op jit(solution)/shard_map/all_gather | solution.py:96
  78.4 36.1 %collective-permute-start = (bf16[2,1024,384]{2,1,0:T(8,128)(2,1)}, bf16[2,1024,384]{2,1,0:T(8,128)(2,1)S(1)}, u32[]{:S(2)}, u32[]{:S(2)}) collective-permute-start(bf16[2,1024,384]{2,1,0:T(8,128)(2,1)} %param.19), channel_id=1, source_target_pairs={{0,1},{1,2},{2,3},{3,0},{4,5},{5,6},{6,7},{7,4},{8,9},{9,10},{10,1... | collective-permute-start | bytes 4718600 | tf_op jit(solution)/shard_map/ppermute | solution.py:85
  114.6 1.1 copy-start.2
  115.7 35.9 %collective-permute-start.1 = (bf16[2,1024,384]{2,1,0:T(8,128)(2,1)S(1)}, bf16[2,1024,384]{2,1,0:T(8,128)(2,1)}, u32[]{:S(2)}, u32[]{:S(2)}) collective-permute-start(bf16[2,1024,384]{2,1,0:T(8,128)(2,1)S(1)} %collective-permute-done), channel_id=1, source_target_pairs={{0,1},{1,2},{2,3},{3,0},{4,5},{5,6},{6,7},{7,4},{8,9},{9,10},{10,1... | collective-permute-start | bytes 4718600 | tf_op jit(solution)/shard_map/ppermute | solution.py:85
  151.6 35.6 %collective-permute-start.2 = (bf16[2,1024,384]{2,1,0:T(8,128)(2,1)}, bf16[2,1024,384]{2,1,0:T(8,128)(2,1)}, u32[]{:S(2)}, u32[]{:S(2)}) collective-permute-start(bf16[2,1024,384]{2,1,0:T(8,128)(2,1)} %collective-permute-done.1), channel_id=1, source_target_pairs={{0,1},{1,2},{2,3},{3,0},{4,5},{5,6},{6,7},{7,4},{8,9},{9,10},{10,1... | collective-permute-start | bytes 4718600 | tf_op jit(solution)/shard_map/ppermute | solution.py:85
  161.5 31.6 %copy-start.3 = (bf16[2,1024,384]{2,1,0:T(8,128)(2,1)S(1)}, bf16[2,1024,384]{2,1,0:T(8,128)(2,1)}, u32[]{:S(2)}) copy-start(bf16[2,1024,384]{2,1,0:T(8,128)(2,1)} %copy-done.2) | copy-start | bytes 4718596
  161.5 33.0 %copy-start.1 = (bf16[2,1024,384]{2,1,0:T(8,128)(2,1)S(1)}, bf16[2,1024,384]{2,1,0:T(8,128)(2,1)}, u32[]{:S(2)}) copy-start(bf16[2,1024,384]{2,1,0:T(8,128)(2,1)} %param.19) | copy-start | bytes 4718596
Sparse Core Ops, SparseCore 0:
  14.5 61.2 all-reduce.4
  79.4 145.9 all-gather.2
